TPU v7x, 32 devices: a whole 2x2x4 slice. The times are simulated.
32 devices in a mesh: groups: 2 (over x), seq: 16 (over z, y, core).
Axes of the slice: x: 2, y: 2, z: 4, core: 2. Of those that a mesh axis runs over, the one named last changes fastest.
Arguments:
- visual: bfloat16 [32768, 1152], P(('groups', 'seq')), parts along dimension 0, may hold values from -18 to 18
- vis_proj: bfloat16 [1152, 1792], replicated, may hold values from -0.1875 to 0.1875
- kv_proj: bfloat16 [1792, 512], replicated, may hold values from -0.125 to 0.125
- out_proj: bfloat16 [1792, 1792], P(None, 'seq'), may hold values from -0.125 to 0.125
- queries: bfloat16 [256, 1792], P(('groups', 'seq')), parts along dimension 0, may hold values from -350 to 350
- frame_range: int32 [2, 2], P('groups'), parts along dimension 0, may hold values from 0 to 64, as said below
- text_lens: int32 [2], P('groups'), parts along dimension 0, may hold values from 1 to 128, as said below
Outputs:
- attended: bfloat16 [256, 1792], P(('groups', 'seq')), parts along dimension 0
There are 2 independent parts, one for each index of `groups`. A program takes and returns all parts, laid end to end along the dimension named above; an argument that names none is the same for every part. Nothing has to cross between parts.
Inputs may be any that keep to these rules, and one draw needn't show every extreme that they name: frame_range[b, 0] < frame_range[b, 1] for every block b; some block attends all 64 frames. `text_lens`: some block is full.
All inputs are finite; a program needn't handle non-finite values.
Results may differ from a plain program's by a relative error of at most 0.02.
The roundings to bfloat16 on the way count: a program that leaves them out, or rounds other values in their place, can miss the bound.
Values may be sent and summed in bfloat16 or wider, within the bound.
A program may use at most 128 MiB of HBM per device.

v0:
```python
import jax
import jax.numpy as jnp
from jax import lax
from jax.sharding import PartitionSpec as P

HEADS = 14
KV_HEADS = 2
HEAD_DIM = 128
FRAME_TOK = 256
QBLK = 128
NEG = -1e30


def fresh_state(row_count):
    return (
        jnp.zeros((row_count, HEADS * HEAD_DIM), jnp.float32),
        jnp.full((row_count, HEADS), NEG, jnp.float32),
        jnp.zeros((row_count, HEADS), jnp.float32),
    )


def absorb(running, query_rows, key_rows, value_rows, allowed):
    output_sum, maxima, totals = running
    row_count = query_rows.shape[0]
    group_size = HEADS // KV_HEADS
    query_heads = query_rows.reshape(row_count, KV_HEADS, group_size, HEAD_DIM)
    scores = jnp.einsum(
        "tkgd,rkd->tkgr", query_heads, key_rows, preferred_element_type=jnp.float32
    ) * HEAD_DIM ** (-0.5)
    masked = jnp.where(allowed, scores, NEG)
    new_maxima = jnp.maximum(maxima, jnp.max(masked, axis=-1).reshape(row_count, HEADS))
    shaped = new_maxima.reshape(row_count, KV_HEADS, group_size)
    weights = jnp.where(allowed, jnp.exp(scores - shaped[..., None]), 0.0)
    new_totals = jnp.sum(weights, axis=-1).reshape(row_count, HEADS)
    blended = jnp.einsum(
        "tkgr,rkd->tkgd",
        weights.astype(jnp.bfloat16),
        value_rows,
        preferred_element_type=jnp.float32,
    )
    new_sum = blended.reshape(row_count, HEADS, HEAD_DIM)
    return (new_sum.reshape(row_count, HEADS * HEAD_DIM), new_maxima, new_totals)


def visit_keys(running, query_rows, key_rows, value_rows, frame_range, block_id, first_row):
    local_count = key_rows.shape[0]
    bounds = lax.dynamic_index_in_dim(frame_range, block_id, 0, keepdims=False)
    frames = (first_row + jnp.arange(local_count, dtype=jnp.int32)) // FRAME_TOK
    allowed = (frames >= bounds[0]) & (frames < bounds[1])
    result = absorb(running, query_rows, key_rows, value_rows, allowed)
    return result


def body(visual, vis_proj, kv_proj, out_proj, queries, frame_range, text_lens):
    devices = lax.axis_size("seq")
    my_index = lax.axis_index("seq")
    hidden = jax.nn.gelu(
        jnp.dot(visual, vis_proj, preferred_element_type=jnp.float32), approximate=True
    ).astype(jnp.bfloat16)
    key_value = jnp.dot(hidden, kv_proj, preferred_element_type=jnp.float32).astype(jnp.bfloat16)
    kv_width = KV_HEADS * HEAD_DIM
    local_count = visual.shape[0]
    key_rows = key_value[:, :kv_width].reshape(local_count, KV_HEADS, HEAD_DIM)
    value_rows = key_value[:, kv_width:].reshape(local_count, KV_HEADS, HEAD_DIM)
    first_row = my_index * local_count
    own_count = queries.shape[0]

    def visit_local(running, query_rows, block_id):
        return visit_keys(
            running, query_rows, key_rows, value_rows, frame_range, block_id, first_row
        )

    every_query = lax.all_gather(queries, "seq", axis=0, tiled=True)
    block_count = every_query.shape[0] // QBLK
    stacked = every_query.reshape(block_count, QBLK, HEADS * HEAD_DIM)

    def one_block(packed):
        block_rows, block_id = packed
        return visit_local(fresh_state(QBLK), block_rows, block_id)

    sums_all, maxima_all, totals_all = lax.map(
        one_block, (stacked, jnp.arange(block_count, dtype=jnp.int32))
    )
    part_sums, part_maxima, part_totals = (
        lax.all_to_all(
            sums_all.reshape(1, block_count * QBLK, HEADS * HEAD_DIM),
            "seq",
            split_axis=1,
            concat_axis=0,
            tiled=True,
        ),
        lax.all_to_all(
            maxima_all.reshape(1, block_count * QBLK, HEADS),
            "seq",
            split_axis=1,
            concat_axis=0,
            tiled=True,
        ),
        lax.all_to_all(
            totals_all.reshape(1, block_count * QBLK, HEADS),
            "seq",
            split_axis=1,
            concat_axis=0,
            tiled=True,
        ),
    )
    maxima = jnp.max(part_maxima, axis=0)
    scaling = jnp.exp(part_maxima - maxima[None])
    totals = jnp.sum(scaling * part_totals, axis=0)
    weighted = part_sums.reshape(devices, own_count, HEADS, HEAD_DIM) * scaling[..., None]
    output_sum = jnp.sum(weighted, axis=0).reshape(own_count, HEADS * HEAD_DIM)
    normed = output_sum.reshape(own_count, HEADS, HEAD_DIM) / totals[..., None]
    my_block = my_index * own_count // QBLK
    length = lax.dynamic_index_in_dim(text_lens, my_block, 0, keepdims=False)
    positions = my_index * own_count % QBLK + jnp.arange(own_count, dtype=jnp.int32)
    attention = (
        jnp.where((positions < length)[:, None, None], normed, 0.0)
        .reshape(own_count, HEADS * HEAD_DIM)
        .astype(jnp.bfloat16)
    )
    return jnp.dot(
        attention,
        lax.all_gather(out_proj, "seq", axis=1, tiled=True),
        preferred_element_type=jnp.float32,
    ).astype(jnp.bfloat16)


def solution(mesh):
    placed = (
        P(("groups", "seq"), None),
        P(),
        P(),
        P(None, "seq"),
        P(("groups", "seq"), None),
        P("groups", None),
        P("groups"),
    )
    return jax.shard_map(
        body, mesh=mesh, in_specs=placed, out_specs=P(("groups", "seq"), None), check_vma=False
    )
```

profile of v0, /device:TPU:9, one launch (start us, length us, event | category | flops | bytes accessed | tf_op | source)
XLA Modules:
  0.0 117.4 jit_solution(4725177874971610116)
XLA Ops:
  6.5 0.7 all-gather.2.cloned.1.call-update
  7.3 22.1 %all_gather.6 = bf16[128,1792]{1,0:T(8,128)(2,1)S(1)} all-gather(bf16[8,1792]{1,0:T(8,128)(2,1)} %param.11), channel_id=1, replica_groups=mesh['groups'=2,'seq'=16] {'seq'}, dimensions={0}, use_global_device_ids=true | all-gather | bytes 487424 | tf_op jit(solution)/shard_map/all_gather | solution.py:73
  29.4 0.3 copy.16
  29.7 1.3 %fusion.39 = (s32[1,1]{1,0:T(1,128)}, s32[1,1]{1,0:T(1,128)}) fusion(s32[1,2]{1,0:T(1,128)} %param.12), kind=kLoop, calls=%fused_computation.51 | loop fusion | bytes 16 | tf_op jit(solution)/shard_map/while/body/eval_jaxpr/slice | solution.py:49
  31.0 1.2 %compare_and_fusion = pred[1024]{0:T(1024)(128)(4,1)S(1)} fusion(s32[]{:T(128)} %bitcast.5, s32[]{:T(128)} %bitcast.4, s32[]{:T(128)S(6)} %mul.69), kind=kLoop, calls=%fused_computation.41 | loop fusion | flops 19456 | bytes 1036 | tf_op jit(solution)/shard_map/while/body/eval_jaxpr/and | solution.py:49
  32.2 11.2 %fusion.18 = bf16[1024,512]{0,1:T(8,128)(2,1)} fusion(bf16[1792,512]{1,0:T(8,128)(2,1)} %param.9, bf16[1024,1152]{1,0:T(8,128)(2,1)S(1)} %copy-done, bf16[1152,1792]{1,0:T(8,128)(2,1)} %param.8), kind=kOutput, calls=%fused_computation.20 | convolution fusion | flops 6123945984 | bytes 9371648 | tf_op jit(solution)/shard_map/dot_general | solution.py:60
  43.4 2.1 %fusion.38 = (bf16[1024,256]{0,1:T(8,128)(2,1)S(1)}, bf16[1024,256]{0,1:T(8,128)(2,1)}) fusion(bf16[1024,512]{0,1:T(8,128)(2,1)} %fusion.18), kind=kLoop, calls=%fused_computation.50 | loop fusion | bytes 2097152 | tf_op jit(solution)/shard_map/slice | solution.py:63
  45.5 1.6 %fusion.8 = (f32[128,2,7]{0,2,1:T(8,128)S(1)}, f32[2,1024,128,7]{2,1,3,0:T(8,128)S(1)}) fusion(pred[1024]{0:T(1024)(128)(4,1)S(1)} %compare_and_fusion, bf16[1024,2,128,1]{0,2,3,1:T(8,128)(2,1)S(1)} %bitcast.58, bf16[128,2,7,128]{0,3,2,1:T(8,128)(2,1)S(1)} %bitcast.59), kind=kOutput, calls=%fused_computation.11 | convolution fusion | flops 475265280 | bytes 8331264 | tf_op jit(solution)/shard_map/while/body/eval_jaxpr/tkgd,rkd->tkgr/dot_general | solution.py:27
  47.1 2.9 %copy-done.1 = f32[2,1024,128,7]{2,1,3,0:T(8,128)} copy-done((f32[2,1024,128,7]{2,1,3,0:T(8,128)}, f32[2,1024,128,7]{2,1,3,0:T(8,128)S(1)}, u32[]{:S(2)}) %copy-start.1) | copy-done | bytes 7340056
  50.1 2.0 %fusion.11 = f32[128,2,7]{0,2,1:T(8,128)S(1)} fusion(f32[2,1024,128,7]{2,1,3,0:T(8,128)S(1)} %get-tuple-element.38, f32[128,2,7]{0,2,1:T(8,128)S(1)} %broadcast_maximum_fusion, pred[1024]{0:T(1024)(128)(4,1)S(1)} %compare_and_fusion), kind=kLoop, calls=%fused_computation.14 | loop fusion | flops 7338240 | bytes 7355392 | tf_op jit(solution)/shard_map/while/body/eval_jaxpr/reduce_sum | solution.py:34
  52.0 0.7 copy.24
  52.8 6.3 %all-to-all-start.2 = ((f32[1,128,14]{2,0,1:T(1,128)}), f32[1,128,14]{2,0,1:T(1,128)S(1)}, u32[]{:S(2)}, u32[]{:S(2)}) async-start(f32[1,128,14]{2,0,1:T(1,128)} %copy.24), calls=%async_computation.2 | async-start | bytes 131072 | tf_op jit(solution)/shard_map/all_to_all | solution.py:99
  59.1 0.7 copy.21
  59.8 4.5 %all-to-all-done.2 = f32[1,128,14]{2,0,1:T(1,128)S(1)} async-done(((f32[1,128,14]{2,0,1:T(1,128)}), f32[1,128,14]{2,0,1:T(1,128)S(1)}, u32[]{:S(2)}, u32[]{:S(2)}) %all-to-all-start.2) | async-done | bytes 7200 | tf_op jit(solution)/shard_map/all_to_all | solution.py:99
  64.3 5.4 %all-to-all-start.1 = ((f32[1,128,14]{2,0,1:T(1,128)}), f32[1,128,14]{2,0,1:T(1,128)S(1)}, u32[]{:S(2)}, u32[]{:S(2)}) async-start(f32[1,128,14]{2,0,1:T(1,128)} %copy.21), calls=%async_computation.1 | async-start | bytes 131072 | tf_op jit(solution)/shard_map/all_to_all | solution.py:92
  69.7 4.8 %fusion.13 = f32[2,128,128,7]{2,1,3,0:T(8,128)S(1)} fusion(bf16[1024,2,128,1]{0,2,3,1:T(8,128)(2,1)} %bitcast.63, f32[2,1024,128,7]{2,1,3,0:T(8,128)} %copy-done.1, f32[128,2,7]{0,2,1:T(8,128)S(1)} %broadcast_maximum_fusion, pred[1024]{0:T(1024)(128)(4,1)S(1)} %compare_and_fusion), kind=kOutput, calls=%fused_computation.16 | convolution fusion | flops 477102080 | bytes 8790016 | tf_op jit(solution)/shard_map/while/body/eval_jaxpr/tkgr,rkd->tkgd/dot_general | solution.py:35
  74.5 2.1 %copy.20 = f32[1,128,1792]{2,0,1:T(1,128)} copy(f32[1,128,1792]{1,2,0:T(8,128)S(1)} %bitcast.60) | data formatting | bytes 1835008 | tf_op jit(solution)/shard_map/while/body/jit(dynamic_update_index_in_dim)/broadcast_in_dim | solution.py:81
  76.6 6.2 %all-to-all-start = ((f32[1,128,1792]{2,0,1:T(1,128)}), f32[1,128,1792]{2,0,1:T(1,128)S(1)}, u32[]{:S(2)}, u32[]{:S(2)}) async-start(f32[1,128,1792]{2,0,1:T(1,128)} %copy.20), calls=%async_computation | async-start | bytes 1835008 | tf_op jit(solution)/shard_map/all_to_all | solution.py:85
  83.4 0.2 copy.33
  83.6 0.8 copy.32
  84.6 0.9 multiply_reduce_fusion
  85.6 19.4 %all-to-all-done = f32[1,128,1792]{2,0,1:T(1,128)S(1)} async-done(((f32[1,128,1792]{2,0,1:T(1,128)}), f32[1,128,1792]{2,0,1:T(1,128)S(1)}, u32[]{:S(2)}, u32[]{:S(2)}) %all-to-all-start) | async-done | bytes 917536 | tf_op jit(solution)/shard_map/all_to_all | solution.py:85
  105.0 0.3 fusion.21
  105.3 5.2 %convolution_convert_fusion = bf16[8,1792]{1,0:T(8,128)(2,1)} fusion(bf16[1792,1792]{0,1:T(8,128)(2,1)} %all-gather.2.cloned.1.call-done, f32[8,1792]{1,0:T(8,128)S(1)} %fusion.21, f32[8,14]{0,1:T(8,128)S(1)} %get-tuple-element.21, pred[8]{0:T(512)(128)(4,1)S(1)} %add_compare_fusion), kind=kOutput, calls=%fused_computation.19 | convolution fusion | flops 51437568 | bytes 6509000 | tf_op jit(solution)/shard_map/dot_general | solution.py:121
  (13 shorter events, 0.2 us)
Async XLA Ops:
  6.5 25.7 %copy-start = (bf16[1024,1152]{1,0:T(8,128)(2,1)S(1)}, bf16[1024,1152]{1,0:T(8,128)(2,1)}, u32[]{:S(2)}) copy-start(bf16[1024,1152]{1,0:T(8,128)(2,1)} %param.7) | copy-start | bytes 7077892
  6.5 98.8 %all-gather.2.cloned.1.call-start = ((), (), s32[]{:S(2)}) async-start(), calls=%async_computation.3 | async-start | bytes 6823936 | tf_op jit(solution)/shard_map/all_gather | solution.py:123
  47.1 3.0 %copy-start.1 = (f32[2,1024,128,7]{2,1,3,0:T(8,128)}, f32[2,1024,128,7]{2,1,3,0:T(8,128)S(1)}, u32[]{:S(2)}) copy-start(f32[2,1024,128,7]{2,1,3,0:T(8,128)S(1)} %get-tuple-element.38) | copy-start | bytes 22020100
  52.8 11.5 %all-to-all-start.2 = ((f32[1,128,14]{2,0,1:T(1,128)}), f32[1,128,14]{2,0,1:T(1,128)S(1)}, u32[]{:S(2)}, u32[]{:S(2)}) async-start(f32[1,128,14]{2,0,1:T(1,128)} %copy.24), calls=%async_computation.2 | async-start | bytes 131072 | tf_op jit(solution)/shard_map/all_to_all | solution.py:99
  64.3 12.3 %all-to-all-start.1 = ((f32[1,128,14]{2,0,1:T(1,128)}), f32[1,128,14]{2,0,1:T(1,128)S(1)}, u32[]{:S(2)}, u32[]{:S(2)}) async-start(f32[1,128,14]{2,0,1:T(1,128)} %copy.21), calls=%async_computation.1 | async-start | bytes 131072 | tf_op jit(solution)/shard_map/all_to_all | solution.py:92
  76.6 28.4 %all-to-all-start = ((f32[1,128,1792]{2,0,1:T(1,128)}), f32[1,128,1792]{2,0,1:T(1,128)S(1)}, u32[]{:S(2)}, u32[]{:S(2)}) async-start(f32[1,128,1792]{2,0,1:T(1,128)} %copy.20), calls=%async_computation | async-start | bytes 1835008 | tf_op jit(solution)/shard_map/all_to_all | solution.py:85
Sparse Core Ops, SparseCore 0:
  9.6 64.7 all-gather.1
where the time goes:
time: 118 us; the launch traced here: 117 us
  waiting for transfers between devices  24.6 us (21%)
  matrix products  22.8 us (19%)
  blocking collectives  22.1 us (19%)
  starting transfers between devices  17.9 us (15%)
  between operations  14.1 us (12%)
  local copies, waits for them, and re-layouts  11.3 us (10%)
  other arithmetic  4.46 us (4%)
    all_gather x1, blocking collectives, body(): every_query = lax.all_gather(queries, 'seq', axis=0, tiled=True)  22.1 us
    all_to_all x1, waiting for transfers between devices, body(): lax.all_to_all(sums_all.reshape(1, block_count * QBLK, HEADS * HEAD_DIM),...  19.4 us
    dot_general x1, matrix products, body(): jnp.dot(hidden, kv_proj, preferred_element_type=jnp.float32)  11.2 us
    all_to_all x1, starting transfers between devices, body(): lax.all_to_all(totals_all.reshape(1, block_count * QBLK, HEADS), 'seq', s...  6.29 us
    all_to_all x1, starting transfers between devices, body(): lax.all_to_all(sums_all.reshape(1, block_count * QBLK, HEADS * HEAD_DIM),...  6.16 us
    all_to_all x1, starting transfers between devices, body(): lax.all_to_all(maxima_all.reshape(1, block_count * QBLK, HEADS), 'seq', s...  5.45 us
    dot_general x1, matrix products, body(): jnp.dot(attention, lax.all_gather(out_proj, 'seq', axis=1, tiled=True), p...  5.24 us
    dot_general x1, matrix products, absorb(): jnp.einsum('tkgr,rkd->tkgd', weights.astype(jnp.bfloat16), value_rows, pr...  4.78 us
  transfers between devices with their start and end apart: 4, of which 2 were waited for; matrix products, arithmetic and copies ran while one was open for 26% of the time, Pallas kernels for 0%

commit v1 on v0

--- a/solution.py
+++ b/solution.py
@@ -70,7 +70,22 @@
             running, query_rows, key_rows, value_rows, frame_range, block_id, first_row
         )
 
-    every_query = lax.all_gather(queries, "seq", axis=0, tiled=True)
+    ways, here, step = (lax.axis_size("seq"), lax.axis_index("seq"), queries.shape[0])
+    dims = [n * ways if d == 0 else n for d, n in enumerate(queries.shape)]
+    every_query = lax.dynamic_update_slice_in_dim(
+        jnp.zeros(dims, queries.dtype), queries, here * step, axis=0
+    )
+    going_up = going_down = queries
+    for far in range(1, ways // 2 + 1):
+        going_up = lax.ppermute(going_up, "seq", [(d, (d + 1) % ways) for d in range(ways)])
+        every_query = lax.dynamic_update_slice_in_dim(
+            every_query, going_up, (here - far) % ways * step, axis=0
+        )
+        if 2 * far < ways:
+            going_down = lax.ppermute(going_down, "seq", [(d, (d - 1) % ways) for d in range(ways)])
+            every_query = lax.dynamic_update_slice_in_dim(
+                every_query, going_down, (here + far) % ways * step, axis=0
+            )
     block_count = every_query.shape[0] // QBLK
     stacked = every_query.reshape(block_count, QBLK, HEADS * HEAD_DIM)
 

time: 118 us -> 285 us (2.42)
  local copies, waits for them, and re-layouts: 11.3 us -> 106 us
  waiting for transfers between devices: 24.6 us -> 87.6 us
  starting transfers between devices: 17.9 us -> 45.1 us
  blocking collectives: 22.1 us -> 0 us
    dynamic_update_slice x0 -> x16, local copies, waits for them, and re-layouts: none -> 94.1 us  [the longest x8 46.8 us: body(): lax.dynamic_update_slice_in_dim(every_query, going_up, (here - far) % way...]
    ppermute x0 -> x15, waiting for transfers between devices: none -> 63.1 us  [the longest x8 34.9 us: body(): lax.ppermute(going_up, 'seq', [(d, (d + 1) % ways) for d in range(ways)])]
    all_gather x1 -> x0, blocking collectives: 22.1 us -> none  [body(): every_query = lax.all_gather(queries, 'seq', axis=0, tiled=True)]
    ppermute x0 -> x15, starting transfers between devices: none -> 20.7 us  [the longest x8 19 us: body(): lax.ppermute(going_up, 'seq', [(d, (d + 1) % ways) for d in range(ways)])]
    all_to_all x1, starting transfers between devices: 6.29 us -> 13.1 us  [body(): lax.all_to_all(totals_all.reshape(1, block_count * QBLK, HEADS), 'seq', s...]
  transfers between devices with their start and end apart: 4 -> 19, of which waited for: 2 -> 13; matrix products, arithmetic and copies ran while one was open for 26% -> 45% of each run, Pallas kernels for 0% -> 0%
where the time goes in v1:
time: 285 us; the launch traced here: 282 us
  local copies, waits for them, and re-layouts  106 us (37%)
  waiting for transfers between devices  87.6 us (31%)
  starting transfers between devices  45.1 us (16%)
  matrix products  23.8 us (8%)
  between operations  14.5 us (5%)
  other arithmetic  4.51 us (2%)
    dynamic_update_slice x8, local copies, waits for them, and re-layouts, body(): lax.dynamic_update_slice_in_dim(every_query, going_up, (here - far) % way...  46.8 us
    dynamic_update_slice x7, local copies, waits for them, and re-layouts, body(): lax.dynamic_update_slice_in_dim(every_query, going_down, (here + far) % w...  41.6 us
    ppermute x8, waiting for transfers between devices, body(): lax.ppermute(going_up, 'seq', [(d, (d + 1) % ways) for d in range(ways)])  34.9 us
    ppermute x7, waiting for transfers between devices, body(): lax.ppermute(going_down, 'seq', [(d, (d - 1) % ways) for d in range(ways)])  28.1 us
    all_to_all x1, waiting for transfers between devices, body(): lax.all_to_all(sums_all.reshape(1, block_count * QBLK, HEADS * HEAD_DIM),...  19.4 us
    ppermute x8, starting transfers between devices, body(): lax.ppermute(going_up, 'seq', [(d, (d + 1) % ways) for d in range(ways)])  19 us
    all_to_all x1, starting transfers between devices, body(): lax.all_to_all(totals_all.reshape(1, block_count * QBLK, HEADS), 'seq', s...  13.1 us
    dot_general x1, matrix products, body(): jnp.dot(hidden, kv_proj, preferred_element_type=jnp.float32)  11.2 us
  transfers between devices with their start and end apart: 19, of which 13 were waited for; matrix products, arithmetic and copies ran while one was open for 45% of the time, Pallas kernels for 0%

profile of v1, /device:TPU:9, one launch (start us, length us, event | category | flops | bytes accessed | tf_op | source)
XLA Modules:
  0.0 281.7 jit_solution(3832703095600176747)
XLA Ops:
  10.2 11.4 %collective-permute-done = bf16[8,1792]{0,1:T(8,128)(2,1)S(1)} collective-permute-done((bf16[8,1792]{0,1:T(8,128)(2,1)S(1)}, bf16[8,1792]{0,1:T(8,128)(2,1)S(1)}, u32[]{:S(2)}, u32[]{:S(2)}) %collective-permute-start) | collective-permute-done | bytes 28704 | tf_op jit(solution)/shard_map/ppermute | solution.py:80
  25.7 6.6 %collective-permute-done.2 = bf16[8,1792]{0,1:T(8,128)(2,1)S(1)} collective-permute-done((bf16[8,1792]{0,1:T(8,128)(2,1)S(1)}, bf16[8,1792]{0,1:T(8,128)(2,1)S(1)}, u32[]{:S(2)}, u32[]{:S(2)}) %collective-permute-start.2) | collective-permute-done | bytes 28704 | tf_op jit(solution)/shard_map/ppermute | solution.py:80
  44.3 9.2 %collective-permute-done.5 = bf16[8,1792]{0,1:T(8,128)(2,1)} collective-permute-done((bf16[8,1792]{0,1:T(8,128)(2,1)S(1)}, bf16[8,1792]{0,1:T(8,128)(2,1)}, u32[]{:S(2)}, u32[]{:S(2)}) %collective-permute-start.5) | collective-permute-done | bytes 28704 | tf_op jit(solution)/shard_map/ppermute | solution.py:85
  53.6 11.7 %collective-permute-done.6 = bf16[8,1792]{0,1:T(8,128)(2,1)} collective-permute-done((bf16[8,1792]{0,1:T(8,128)(2,1)S(1)}, bf16[8,1792]{0,1:T(8,128)(2,1)}, u32[]{:S(2)}, u32[]{:S(2)}) %collective-permute-start.6) | collective-permute-done | bytes 28704 | tf_op jit(solution)/shard_map/ppermute | solution.py:80
  68.2 11.2 %fusion.18 = bf16[1024,512]{0,1:T(8,128)(2,1)} fusion(bf16[1792,512]{1,0:T(8,128)(2,1)} %param.9, bf16[1024,1152]{1,0:T(8,128)(2,1)S(1)} %copy-done, bf16[1152,1792]{1,0:T(8,128)(2,1)} %param.8), kind=kOutput, calls=%fused_computation.20 | convolution fusion | flops 6123945984 | bytes 9371648 | tf_op jit(solution)/shard_map/dot_general | solution.py:60
  93.7 10.6 %collective-permute-done.11 = bf16[8,1792]{0,1:T(8,128)(2,1)} collective-permute-done((bf16[8,1792]{0,1:T(8,128)(2,1)}, bf16[8,1792]{0,1:T(8,128)(2,1)}, u32[]{:S(2)}, u32[]{:S(2)}) %collective-permute-start.11) | collective-permute-done | bytes 28704 | tf_op jit(solution)/shard_map/ppermute | solution.py:85
  108.4 5.7 %dynamic_update_slice.88 = bf16[128,1792]{0,1:T(8,128)(2,1)} dynamic-update-slice(bf16[128,1792]{0,1:T(8,128)(2,1)} %squeeze.26, bf16[8,1792]{0,1:T(8,128)(2,1)S(1)} %copy.18, s32[]{:T(128)S(6)} %select_n.144, s32[]{:T(128)} %constant.188.clone.1) | dynamic-update-slice | bytes 57348 | tf_op jit(solution)/shard_map/dynamic_update_slice | solution.py:75
  114.1 5.9 %dynamic_update_slice.89 = bf16[128,1792]{0,1:T(8,128)(2,1)} dynamic-update-slice(bf16[128,1792]{0,1:T(8,128)(2,1)} %dynamic_update_slice.88, bf16[8,1792]{0,1:T(8,128)(2,1)} %copy-done.2, s32[]{:T(128)S(6)} %select_n.146, s32[]{:T(128)} %constant.188.clone.1) | dynamic-update-slice | bytes 57348 | tf_op jit(solution)/shard_map/dynamic_update_slice | solution.py:81
  120.1 5.9 %dynamic_update_slice.90 = bf16[128,1792]{0,1:T(8,128)(2,1)} dynamic-update-slice(bf16[128,1792]{0,1:T(8,128)(2,1)} %dynamic_update_slice.89, bf16[8,1792]{0,1:T(8,128)(2,1)} %copy-done.3, s32[]{:T(128)S(6)} %select_n.148, s32[]{:T(128)} %constant.188.clone.1) | dynamic-update-slice | bytes 57348 | tf_op jit(solution)/shard_map/dynamic_update_slice | solution.py:86
  126.0 5.9 %dynamic_update_slice.91 = bf16[128,1792]{0,1:T(8,128)(2,1)} dynamic-update-slice(bf16[128,1792]{0,1:T(8,128)(2,1)} %dynamic_update_slice.90, bf16[8,1792]{0,1:T(8,128)(2,1)} %copy-done.4, s32[]{:T(128)S(6)} %select_n.150, s32[]{:T(128)} %constant.188.clone.1) | dynamic-update-slice | bytes 57348 | tf_op jit(solution)/shard_map/dynamic_update_slice | solution.py:81
  132.0 5.9 %dynamic_update_slice.92 = bf16[128,1792]{0,1:T(8,128)(2,1)} dynamic-update-slice(bf16[128,1792]{0,1:T(8,128)(2,1)} %dynamic_update_slice.91, bf16[8,1792]{0,1:T(8,128)(2,1)} %copy-done.5, s32[]{:T(128)S(6)} %select_n.152, s32[]{:T(128)} %constant.188.clone.1) | dynamic-update-slice | bytes 57348 | tf_op jit(solution)/shard_map/dynamic_update_slice | solution.py:86
  137.9 5.9 %dynamic_update_slice.93 = bf16[128,1792]{0,1:T(8,128)(2,1)} dynamic-update-slice(bf16[128,1792]{0,1:T(8,128)(2,1)} %dynamic_update_slice.92, bf16[8,1792]{0,1:T(8,128)(2,1)} %copy-done.6, s32[]{:T(128)S(6)} %select_n.154, s32[]{:T(128)} %constant.188.clone.1) | dynamic-update-slice | bytes 57348 | tf_op jit(solution)/shard_map/dynamic_update_slice | solution.py:81
  143.9 5.9 %dynamic_update_slice.94 = bf16[128,1792]{0,1:T(8,128)(2,1)} dynamic-update-slice(bf16[128,1792]{0,1:T(8,128)(2,1)} %dynamic_update_slice.93, bf16[8,1792]{0,1:T(8,128)(2,1)} %collective-permute-done.5, s32[]{:T(128)S(6)} %select_n.156, s32[]{:T(128)} %constant.188.clone.1) | dynamic-update-slice | bytes 57348 | tf_op jit(solution)/shard_map/dynamic_update_slice | solution.py:86
  149.8 5.9 %dynamic_update_slice.95 = bf16[128,1792]{0,1:T(8,128)(2,1)} dynamic-update-slice(bf16[128,1792]{0,1:T(8,128)(2,1)} %dynamic_update_slice.94, bf16[8,1792]{0,1:T(8,128)(2,1)} %collective-permute-done.6, s32[]{:T(128)S(6)} %select_n.158, s32[]{:T(128)} %constant.188.clone.1) | dynamic-update-slice | bytes 57348 | tf_op jit(solution)/shard_map/dynamic_update_slice | solution.py:81
  155.8 5.9 %dynamic_update_slice.96 = bf16[128,1792]{0,1:T(8,128)(2,1)} dynamic-update-slice(bf16[128,1792]{0,1:T(8,128)(2,1)} %dynamic_update_slice.95, bf16[8,1792]{0,1:T(8,128)(2,1)} %collective-permute-done.7, s32[]{:T(128)S(6)} %select_n.160, s32[]{:T(128)} %constant.188.clone.1) | dynamic-update-slice | bytes 57348 | tf_op jit(solution)/shard_map/dynamic_update_slice | solution.py:86
  166.8 5.9 %dynamic_update_slice.98 = bf16[128,1792]{0,1:T(8,128)(2,1)} dynamic-update-slice(bf16[128,1792]{0,1:T(8,128)(2,1)} %dynamic_update_slice.97, bf16[8,1792]{0,1:T(8,128)(2,1)} %collective-permute-done.9, s32[]{:T(128)S(6)} %select_n.164, s32[]{:T(128)} %constant.188.clone.1) | dynamic-update-slice | bytes 57348 | tf_op jit(solution)/shard_map/dynamic_update_slice | solution.py:86
  172.8 5.9 %dynamic_update_slice.99 = bf16[128,1792]{0,1:T(8,128)(2,1)} dynamic-update-slice(bf16[128,1792]{0,1:T(8,128)(2,1)} %dynamic_update_slice.98, bf16[8,1792]{0,1:T(8,128)(2,1)} %collective-permute-done.10, s32[]{:T(128)S(6)} %select_n.166, s32[]{:T(128)} %constant.188.clone.1) | dynamic-update-slice | bytes 57348 | tf_op jit(solution)/shard_map/dynamic_update_slice | solution.py:81
  178.7 5.9 %dynamic_update_slice.100 = bf16[128,1792]{0,1:T(8,128)(2,1)} dynamic-update-slice(bf16[128,1792]{0,1:T(8,128)(2,1)} %dynamic_update_slice.99, bf16[8,1792]{0,1:T(8,128)(2,1)} %collective-permute-done.11, s32[]{:T(128)S(6)} %select_n.168, s32[]{:T(128)} %constant.188.clone.1) | dynamic-update-slice | bytes 57348 | tf_op jit(solution)/shard_map/dynamic_update_slice | solution.py:86
  184.7 5.9 %dynamic_update_slice.101 = bf16[128,1792]{0,1:T(8,128)(2,1)} dynamic-update-slice(bf16[128,1792]{0,1:T(8,128)(2,1)} %dynamic_update_slice.100, bf16[8,1792]{0,1:T(8,128)(2,1)} %collective-permute-done.12, s32[]{:T(128)S(6)} %select_n.170, s32[]{:T(128)} %constant.188.clone.1) | dynamic-update-slice | bytes 57348 | tf_op jit(solution)/shard_map/dynamic_update_slice | solution.py:81
  190.6 6.0 %dynamic_update_slice.102 = bf16[128,1792]{0,1:T(8,128)(2,1)} dynamic-update-slice(bf16[128,1792]{0,1:T(8,128)(2,1)} %dynamic_update_slice.101, bf16[8,1792]{0,1:T(8,128)(2,1)} %collective-permute-done.13, s32[]{:T(128)S(6)} %select_n.172, s32[]{:T(128)} %constant.188.clone.1) | dynamic-update-slice | bytes 57348 | tf_op jit(solution)/shard_map/dynamic_update_slice | solution.py:86
  196.6 6.0 %dynamic_update_slice.103 = bf16[128,1792]{0,1:T(8,128)(2,1)} dynamic-update-slice(bf16[128,1792]{0,1:T(8,128)(2,1)} %dynamic_update_slice.102, bf16[8,1792]{0,1:T(8,128)(2,1)} %collective-permute-done.14, s32[]{:T(128)S(6)} %select_n.174, s32[]{:T(128)} %constant.188.clone.1) | dynamic-update-slice | bytes 57348 | tf_op jit(solution)/shard_map/dynamic_update_slice | solution.py:81
  210.9 13.1 %all-to-all-start.2 = ((f32[1,128,14]{2,0,1:T(1,128)}), f32[1,128,14]{2,0,1:T(1,128)S(1)}, u32[]{:S(2)}, u32[]{:S(2)}) async-start(f32[1,128,14]{2,0,1:T(1,128)} %copy.28), calls=%async_computation.2 | async-start | bytes 131072 | tf_op jit(solution)/shard_map/all_to_all | solution.py:114
  241.0 6.1 %all-to-all-start = ((f32[1,128,1792]{2,0,1:T(1,128)}), f32[1,128,1792]{2,0,1:T(1,128)S(1)}, u32[]{:S(2)}, u32[]{:S(2)}) async-start(f32[1,128,1792]{2,0,1:T(1,128)} %copy.24), calls=%async_computation | async-start | bytes 1835008 | tf_op jit(solution)/shard_map/all_to_all | solution.py:100
  249.9 19.4 %all-to-all-done = f32[1,128,1792]{2,0,1:T(1,128)S(1)} async-done(((f32[1,128,1792]{2,0,1:T(1,128)}), f32[1,128,1792]{2,0,1:T(1,128)S(1)}, u32[]{:S(2)}, u32[]{:S(2)}) %all-to-all-start) | async-done | bytes 917536 | tf_op jit(solution)/shard_map/all_to_all | solution.py:100
  (71 shorter events, 79.0 us)
Async XLA Ops:
  6.5 61.6 %copy-start = (bf16[1024,1152]{1,0:T(8,128)(2,1)S(1)}, bf16[1024,1152]{1,0:T(8,128)(2,1)}, u32[]{:S(2)}) copy-start(bf16[1024,1152]{1,0:T(8,128)(2,1)} %param.7) | copy-start | bytes 7077892
  6.5 263.1 %all-gather.2.cloned.1.call-start = ((), (), s32[]{:S(2)}) async-start(), calls=%async_computation.3 | async-start | bytes 6823936 | tf_op jit(solution)/shard_map/all_gather | solution.py:138
  8.3 84.7 %copy-start.7 = (s32[1,2]{1,0:T(1,128)S(1)}, s32[1,2]{1,0:T(1,128)}, u32[]{:S(2)}) copy-start(s32[1,2]{1,0:T(1,128)} %param.12) | copy-start | bytes 28
  8.3 13.3 %collective-permute-start = (bf16[8,1792]{0,1:T(8,128)(2,1)S(1)}, bf16[8,1792]{0,1:T(8,128)(2,1)S(1)}, u32[]{:S(2)}, u32[]{:S(2)}) collective-permute-start(bf16[8,1792]{0,1:T(8,128)(2,1)S(1)} %copy.18), channel_id=1, source_target_pairs={{0,1},{1,2},{2,3},{3,4},{4,5},{5,6},{6,7},{7,8},{8,9},{9,10},{10,1... | collective-permute-start | bytes 86024 | tf_op jit(solution)/shard_map/ppermute | solution.py:80
  10.2 15.6 %collective-permute-start.1 = (bf16[8,1792]{0,1:T(8,128)(2,1)S(1)}, bf16[8,1792]{0,1:T(8,128)(2,1)S(1)}, u32[]{:S(2)}, u32[]{:S(2)}) collective-permute-start(bf16[8,1792]{0,1:T(8,128)(2,1)S(1)} %copy.18), channel_id=1, source_target_pairs={{0,15},{1,0},{2,1},{3,2},{4,3},{5,4},{6,5},{7,6},{8,7},{9,8},{10,9... | collective-permute-start | bytes 86024 | tf_op jit(solution)/shard_map/ppermute | solution.py:85
  21.6 57.8 %copy-start.2 = (bf16[8,1792]{0,1:T(8,128)(2,1)}, bf16[8,1792]{0,1:T(8,128)(2,1)S(1)}, u32[]{:S(2)}) copy-start(bf16[8,1792]{0,1:T(8,128)(2,1)S(1)} %collective-permute-done) | copy-start | bytes 86020
  21.6 10.7 %collective-permute-start.2 = (bf16[8,1792]{0,1:T(8,128)(2,1)S(1)}, bf16[8,1792]{0,1:T(8,128)(2,1)S(1)}, u32[]{:S(2)}, u32[]{:S(2)}) collective-permute-start(bf16[8,1792]{0,1:T(8,128)(2,1)S(1)} %collective-permute-done), channel_id=1, source_target_pairs={{0,1},{1,2},{2,3},{3,4},{4,5},{5,6},{6,7},{7,8},{8,9},{9,10},{10,1... | collective-permute-start | bytes 86024 | tf_op jit(solution)/shard_map/ppermute | solution.py:80
  25.7 6.6 %copy-start.3 = (bf16[8,1792]{0,1:T(8,128)(2,1)}, bf16[8,1792]{0,1:T(8,128)(2,1)S(1)}, u32[]{:S(2)}) copy-start(bf16[8,1792]{0,1:T(8,128)(2,1)S(1)} %collective-permute-done.1) | copy-start | bytes 86020
  25.7 10.9 %collective-permute-start.3 = (bf16[8,1792]{0,1:T(8,128)(2,1)S(1)}, bf16[8,1792]{0,1:T(8,128)(2,1)S(1)}, u32[]{:S(2)}, u32[]{:S(2)}) collective-permute-start(bf16[8,1792]{0,1:T(8,128)(2,1)S(1)} %collective-permute-done.1), channel_id=1, source_target_pairs={{0,15},{1,0},{2,1},{3,2},{4,3},{5,4},{6,5},{7,6},{8,7},{9,8},{10,9... | collective-permute-start | bytes 86024 | tf_op jit(solution)/shard_map/ppermute | solution.py:85
  32.3 9.5 %collective-permute-start.4 = (bf16[8,1792]{0,1:T(8,128)(2,1)S(1)}, bf16[8,1792]{0,1:T(8,128)(2,1)S(1)}, u32[]{:S(2)}, u32[]{:S(2)}) collective-permute-start(bf16[8,1792]{0,1:T(8,128)(2,1)S(1)} %collective-permute-done.2), channel_id=1, source_target_pairs={{0,1},{1,2},{2,3},{3,4},{4,5},{5,6},{6,7},{7,8},{8,9},{9,10},{10,1... | collective-permute-start | bytes 86024 | tf_op jit(solution)/shard_map/ppermute | solution.py:80
  36.6 16.9 %collective-permute-start.5 = (bf16[8,1792]{0,1:T(8,128)(2,1)S(1)}, bf16[8,1792]{0,1:T(8,128)(2,1)}, u32[]{:S(2)}, u32[]{:S(2)}) collective-permute-start(bf16[8,1792]{0,1:T(8,128)(2,1)S(1)} %collective-permute-done.3), channel_id=1, source_target_pairs={{0,15},{1,0},{2,1},{3,2},{4,3},{5,4},{6,5},{7,6},{8,7},{9,8},{10,9... | collective-permute-start | bytes 86024 | tf_op jit(solution)/shard_map/ppermute | solution.py:85
  41.9 11.7 %copy-start.6 = (bf16[8,1792]{0,1:T(8,128)(2,1)}, bf16[8,1792]{0,1:T(8,128)(2,1)S(1)}, u32[]{:S(2)}) copy-start(bf16[8,1792]{0,1:T(8,128)(2,1)S(1)} %collective-permute-done.4) | copy-start | bytes 86020
  41.9 23.4 %collective-permute-start.6 = (bf16[8,1792]{0,1:T(8,128)(2,1)S(1)}, bf16[8,1792]{0,1:T(8,128)(2,1)}, u32[]{:S(2)}, u32[]{:S(2)}) collective-permute-start(bf16[8,1792]{0,1:T(8,128)(2,1)S(1)} %collective-permute-done.4), channel_id=1, source_target_pairs={{0,1},{1,2},{2,3},{3,4},{4,5},{5,6},{6,7},{7,8},{8,9},{9,10},{10,1... | collective-permute-start | bytes 86024 | tf_op jit(solution)/shard_map/ppermute | solution.py:80
  53.6 25.8 %collective-permute-start.7 = (bf16[8,1792]{0,1:T(8,128)(2,1)}, bf16[8,1792]{0,1:T(8,128)(2,1)}, u32[]{:S(2)}, u32[]{:S(2)}) collective-permute-start(bf16[8,1792]{0,1:T(8,128)(2,1)} %collective-permute-done.5), channel_id=1, source_target_pairs={{0,15},{1,0},{2,1},{3,2},{4,3},{5,4},{6,5},{7,6},{8,7},{9,8},{10,9... | collective-permute-start | bytes 86024 | tf_op jit(solution)/shard_map/ppermute | solution.py:85
  65.2 15.7 %collective-permute-start.8 = (bf16[8,1792]{0,1:T(8,128)(2,1)}, bf16[8,1792]{0,1:T(8,128)(2,1)}, u32[]{:S(2)}, u32[]{:S(2)}) collective-permute-start(bf16[8,1792]{0,1:T(8,128)(2,1)} %collective-permute-done.6), channel_id=1, source_target_pairs={{0,1},{1,2},{2,3},{3,4},{4,5},{5,6},{6,7},{7,8},{8,9},{9,10},{10,1... | collective-permute-start | bytes 86024 | tf_op jit(solution)/shard_map/ppermute | solution.py:80
  79.4 11.0 %collective-permute-start.9 = (bf16[8,1792]{0,1:T(8,128)(2,1)}, bf16[8,1792]{0,1:T(8,128)(2,1)}, u32[]{:S(2)}, u32[]{:S(2)}) collective-permute-start(bf16[8,1792]{0,1:T(8,128)(2,1)} %collective-permute-done.7), channel_id=1, source_target_pairs={{0,15},{1,0},{2,1},{3,2},{4,3},{5,4},{6,5},{7,6},{8,7},{9,8},{10,9... | collective-permute-start | bytes 86024 | tf_op jit(solution)/shard_map/ppermute | solution.py:85
  81.0 9.6 %collective-permute-start.10 = (bf16[8,1792]{0,1:T(8,128)(2,1)}, bf16[8,1792]{0,1:T(8,128)(2,1)}, u32[]{:S(2)}, u32[]{:S(2)}) collective-permute-start(bf16[8,1792]{0,1:T(8,128)(2,1)} %collective-permute-done.8), channel_id=1, source_target_pairs={{0,1},{1,2},{2,3},{3,4},{4,5},{5,6},{6,7},{7,8},{8,9},{9,10},{10,1... | collective-permute-start | bytes 86024 | tf_op jit(solution)/shard_map/ppermute | solution.py:80
  90.3 14.0 %collective-permute-start.11 = (bf16[8,1792]{0,1:T(8,128)(2,1)}, bf16[8,1792]{0,1:T(8,128)(2,1)}, u32[]{:S(2)}, u32[]{:S(2)}) collective-permute-start(bf16[8,1792]{0,1:T(8,128)(2,1)} %collective-permute-done.9), channel_id=1, source_target_pairs={{0,15},{1,0},{2,1},{3,2},{4,3},{5,4},{6,5},{7,6},{8,7},{9,8},{10,9... | collective-permute-start | bytes 86024 | tf_op jit(solution)/shard_map/ppermute | solution.py:85
  90.5 13.8 %collective-permute-start.12 = (bf16[8,1792]{0,1:T(8,128)(2,1)}, bf16[8,1792]{0,1:T(8,128)(2,1)}, u32[]{:S(2)}, u32[]{:S(2)}) collective-permute-start(bf16[8,1792]{0,1:T(8,128)(2,1)} %collective-permute-done.10), channel_id=1, source_target_pairs={{0,1},{1,2},{2,3},{3,4},{4,5},{5,6},{6,7},{7,8},{8,9},{9,10},{10,1... | collective-permute-start | bytes 86024 | tf_op jit(solution)/shard_map/ppermute | solution.py:80
  104.3 86.3 %collective-permute-start.13 = (bf16[8,1792]{0,1:T(8,128)(2,1)}, bf16[8,1792]{0,1:T(8,128)(2,1)}, u32[]{:S(2)}, u32[]{:S(2)}) collective-permute-start(bf16[8,1792]{0,1:T(8,128)(2,1)} %collective-permute-done.11), channel_id=1, source_target_pairs={{0,15},{1,0},{2,1},{3,2},{4,3},{5,4},{6,5},{7,6},{8,7},{9,8},{10,9... | collective-permute-start | bytes 86024 | tf_op jit(solution)/shard_map/ppermute | solution.py:85
  104.3 92.3 %collective-permute-start.14 = (bf16[8,1792]{0,1:T(8,128)(2,1)}, bf16[8,1792]{0,1:T(8,128)(2,1)}, u32[]{:S(2)}, u32[]{:S(2)}) collective-permute-start(bf16[8,1792]{0,1:T(8,128)(2,1)} %collective-permute-done.12), channel_id=1, source_target_pairs={{0,1},{1,2},{2,3},{3,4},{4,5},{5,6},{6,7},{7,8},{8,9},{9,10},{10,1... | collective-permute-start | bytes 86024 | tf_op jit(solution)/shard_map/ppermute | solution.py:80
  210.9 18.2 %all-to-all-start.2 = ((f32[1,128,14]{2,0,1:T(1,128)}), f32[1,128,14]{2,0,1:T(1,128)S(1)}, u32[]{:S(2)}, u32[]{:S(2)}) async-start(f32[1,128,14]{2,0,1:T(1,128)} %copy.28), calls=%async_computation.2 | async-start | bytes 131072 | tf_op jit(solution)/shard_map/all_to_all | solution.py:114
  229.0 12.0 %all-to-all-start.1 = ((f32[1,128,14]{2,0,1:T(1,128)}), f32[1,128,14]{2,0,1:T(1,128)S(1)}, u32[]{:S(2)}, u32[]{:S(2)}) async-start(f32[1,128,14]{2,0,1:T(1,128)} %copy.25), calls=%async_computation.1 | async-start | bytes 131072 | tf_op jit(solution)/shard_map/all_to_all | solution.py:107
  241.0 28.3 %all-to-all-start = ((f32[1,128,1792]{2,0,1:T(1,128)}), f32[1,128,1792]{2,0,1:T(1,128)S(1)}, u32[]{:S(2)}, u32[]{:S(2)}) async-start(f32[1,128,1792]{2,0,1:T(1,128)} %copy.24), calls=%async_computation | async-start | bytes 1835008 | tf_op jit(solution)/shard_map/all_to_all | solution.py:100
  (3 other events, 12.5 us)
Sparse Core Ops, SparseCore 0:
  9.6 89.0 all-gather.1
